TPU v7x, 32 devices: a whole 2x2x4 slice. The times are simulated.
32 devices in a mesh: ctx: 16 (over z, y, x), wsh: 2 (over core).
Axes of the slice: x: 2, y: 2, z: 4, core: 2. Of those that a mesh axis runs over, the one named last changes fastest.
Arguments:
- tokens: bfloat16 [8, 2048, 512], P('wsh', 'ctx'), may hold values from -6 to 6
- routes: int32 [8, 2048, 2], P('wsh', 'ctx'), may hold values from 0 to 7, all different within a row
- block_order: int32 [16], replicated, may hold values from 0 to 15, each once
- norm_gain1: bfloat16 [512], P('wsh'), may hold values from 0.5 to 1.5
- router_w: bfloat16 [512, 8], P('wsh'), may hold values from -0.1875 to 0.1875
- query_w: bfloat16 [512, 512], P('wsh'), may hold values from -0.25 to 0.25
- kv_w: bfloat16 [512, 128], P('wsh'), may hold values from -0.25 to 0.25
- out_w: bfloat16 [512, 512], P('wsh'), may hold values from -6 to 6
- norm_gain2: bfloat16 [512], P('wsh'), may hold values from 0.5 to 1.5
- up_w: bfloat16 [512, 2048], P('wsh'), may hold values from -0.25 to 0.25
- down_w: bfloat16 [2048, 512], P('wsh'), may hold values from -0.125 to 0.125
- cotangent: bfloat16 [8, 2048, 512], P('wsh', 'ctx'), may hold values from -6 to 6
Outputs:
- layer_out: float32 [8, 2048, 512], P('wsh', 'ctx')
- input_grad: float32 [8, 2048, 512], P('wsh', 'ctx')
- grad_gain1: float32 [512], P('wsh')
- grad_router: float32 [512, 8], P('wsh')
- grad_query: float32 [512, 512], P('wsh')
- grad_kv: float32 [512, 128], P('wsh')
- grad_out: float32 [512, 512], P('wsh')
- grad_gain2: float32 [512], P('wsh')
- grad_up: float32 [512, 2048], P('wsh')
- grad_down: float32 [2048, 512], P('wsh')
Inputs may be any that keep to these rules, and one draw needn't show every extreme that they name: `routes`: each token names 2 different experts. A permutation: index p of ctx holds, of every sequence, block block_order[p] and block 31 - block_order[p], as the first step says.
All inputs are finite; a program needn't handle non-finite values.
Results may differ from a plain program's by a relative error of at most 0.013.
Values may be sent and summed in bfloat16 or wider, within the bound.
No kernel may reach another device: no remote copies, remote signals or barrier semaphores. Data moves between devices by JAX's collectives and lax.ppermute only.
A program may use at most 192 MiB of HBM per device.

v0:
```python
import math
import jax
import jax.numpy as jnp
from jax import lax
from jax.sharding import PartitionSpec as P

MB = 4
HIGHEST = lax.Precision.HIGHEST


def smooth_unit(values_in):
    return jax.nn.gelu(values_in, approximate=False)


def normalize(inputs, gain_vec):
    centre = inputs - jnp.mean(inputs, axis=-1, keepdims=True)
    spread = jnp.mean(centre * centre, axis=-1, keepdims=True)
    return centre * lax.rsqrt(spread + 1e-05) * gain_vec


def gating(logits, expert_hot):
    chosen = jnp.sum(expert_hot * logits[..., None, :], axis=-1)
    return jax.nn.softmax(chosen, axis=-1)


def tile_scores(queries, kv_all, query_places, key_places, first_row, width):
    head = queries.shape[-1]
    tile = lax.dynamic_slice_in_dim(kv_all, first_row, width, 1)
    places = lax.dynamic_slice_in_dim(key_places, first_row, width, 0)
    keys_tile = tile[..., :head]
    values_tile = tile[..., head:]
    scores = jnp.einsum("btsh,bkh->btsk", queries, keys_tile, preferred_element_type=jnp.float32)
    allowed = places[None, None, None, :] <= query_places[None, :, None, None]
    return (keys_tile, values_tile, scores, allowed)


def log_totals(queries, kv_all, query_places, key_places):
    rows = kv_all.shape[1]
    width = math.gcd(rows, 2048)

    def log_advance(carry, index):
        top_score, total = carry
        unused_keys, unused_values, scores, allowed = tile_scores(
            queries, kv_all, query_places, key_places, index * width, width
        )
        fresh = jnp.maximum(top_score, jnp.max(jnp.where(allowed, scores, -1e30), axis=-1))
        shares = jnp.where(allowed, jnp.exp(scores - fresh[..., None]), 0.0)
        total = total * jnp.exp(top_score - fresh) + jnp.sum(shares, axis=-1)
        return ((fresh, total), None)

    shape = queries.shape[:-1]
    initial = (jnp.full(shape, -1e30, jnp.float32), jnp.zeros(shape, jnp.float32))
    carry, unused = lax.scan(log_advance, initial, jnp.arange(rows // width, dtype=jnp.int32))
    return carry[0] + jnp.log(carry[1])


def attend(queries, kv_all, query_places, key_places, log_total):
    rows = kv_all.shape[1]
    width = math.gcd(rows, 2048)

    def attend_advance(carry, index):
        unused_keys, values_tile, scores, allowed = tile_scores(
            queries, kv_all, query_places, key_places, index * width, width
        )
        shares = jnp.where(allowed, jnp.exp(scores - log_total[..., None]), 0.0).astype(
            jnp.bfloat16
        )
        return (
            carry
            + jnp.einsum("btsk,bkh->btsh", shares, values_tile, preferred_element_type=jnp.float32),
            None,
        )

    summed, unused = lax.scan(
        attend_advance,
        jnp.zeros(queries.shape, jnp.float32),
        jnp.arange(rows // width, dtype=jnp.int32),
    )
    return summed


def key_range_grads(
    queries, back_attended, kv_all, query_places, key_places, log_total, row_delta, begin, row_count
):
    width = math.gcd(row_count, 2048)

    def key_advance(carry, index):
        back_query, back_kv = carry
        keys_tile, values_tile, scores, allowed = tile_scores(
            queries, kv_all, query_places, key_places, begin + index * width, width
        )
        shares = jnp.where(allowed, jnp.exp(scores - log_total[..., None]), 0.0)
        back_shares = jnp.einsum(
            "btsh,bkh->btsk", back_attended, values_tile, preferred_element_type=jnp.float32
        )
        back_scores = (shares * (back_shares - row_delta[..., None])).astype(jnp.bfloat16)
        back_query = back_query + jnp.einsum(
            "btsk,bkh->btsh", back_scores, keys_tile, preferred_element_type=jnp.float32
        )
        back_keys = jnp.einsum(
            "btsk,btsh->bkh", back_scores, queries, preferred_element_type=jnp.float32
        )
        back_values = jnp.einsum(
            "btsk,btsh->bkh",
            shares.astype(jnp.bfloat16),
            back_attended,
            preferred_element_type=jnp.float32,
        )
        back_kv = lax.dynamic_update_slice_in_dim(
            back_kv, jnp.concatenate([back_keys, back_values], axis=-1), index * width, 1
        )
        return ((back_query, back_kv), None)

    head = queries.shape[-1]
    kv_start = jnp.zeros((queries.shape[0], row_count, 2 * head), jnp.float32)
    carry, unused = lax.scan(
        key_advance,
        (jnp.zeros(queries.shape, jnp.float32), kv_start),
        jnp.arange(row_count // width, dtype=jnp.int32),
    )
    return carry


def on_device(
    tokens,
    routes,
    block_order,
    norm_gain1,
    router_w,
    query_w,
    kv_w,
    out_w,
    norm_gain2,
    up_w,
    down_w,
    cotangent,
):
    gathered = (
        lax.all_gather(norm_gain1, "wsh", axis=0, tiled=True),
        lax.all_gather(router_w, "wsh", axis=0, tiled=True),
        lax.all_gather(query_w, "wsh", axis=0, tiled=True),
        lax.all_gather(kv_w, "wsh", axis=0, tiled=True),
        lax.all_gather(out_w, "wsh", axis=0, tiled=True),
        lax.all_gather(norm_gain2, "wsh", axis=0, tiled=True),
        lax.all_gather(up_w, "wsh", axis=0, tiled=True),
        lax.all_gather(down_w, "wsh", axis=0, tiled=True),
    )
    gain_one, router, query_mat, kv_mat, out_mat, gain_two, up_mat, down_mat = gathered
    gain_one_f = gain_one.astype(jnp.float32)
    gain_two_f = gain_two.astype(jnp.float32)
    router_f = router.astype(jnp.float32)
    experts = router.shape[1]
    head = kv_mat.shape[1] // 2
    pairs = lax.axis_size("ctx")
    local = tokens.shape[1]
    block = local // 2
    offsets = jnp.arange(block, dtype=jnp.int32)
    front_rows = block_order[:, None] * block + offsets[None, :]
    back_rows = (2 * pairs - 1 - block_order)[:, None] * block + offsets[None, :]
    key_places = jnp.concatenate([front_rows, back_rows], axis=1).reshape(-1)
    length = key_places.shape[0]
    query_places = lax.dynamic_slice_in_dim(key_places, lax.axis_index("ctx") * local, local, 0)
    group = tokens.shape[0] // MB
    totals = [jnp.zeros(w.shape, jnp.float32) for w in gathered]
    layer_parts = []
    input_parts = []
    for batch in range(MB):
        inputs = tokens[batch * group : (batch + 1) * group].astype(jnp.float32)
        seq_routes = routes[batch * group : (batch + 1) * group]
        seq_cotangent = cotangent[batch * group : (batch + 1) * group]
        seqs = inputs.shape[0]
        expert_hot = (seq_routes[..., None] == jnp.arange(experts, dtype=jnp.int32)).astype(
            jnp.float32
        )
        normed, norm_pull_one = jax.vjp(normalize, inputs, gain_one_f)
        normed_low = normed.astype(jnp.bfloat16)
        logits = jnp.dot(normed_low, router, preferred_element_type=jnp.float32)
        gate_values, gate_pull = jax.vjp(lambda values_in: gating(values_in, expert_hot), logits)
        query_all = jnp.dot(normed_low, query_mat, preferred_element_type=jnp.float32).reshape(
            seqs, local, experts, head
        )
        queries = (
            jnp.einsum("btse,bteh->btsh", expert_hot, query_all, precision=HIGHEST) * 0.125
        ).astype(jnp.bfloat16)
        keyval = jnp.dot(normed_low, kv_mat, preferred_element_type=jnp.float32).astype(
            jnp.bfloat16
        )
        kv_all = lax.all_gather(keyval, "ctx", axis=1, tiled=True)
        log_total = log_totals(queries, kv_all, query_places, key_places)
        attended = attend(queries, kv_all, query_places, key_places, log_total)
        weighted = gate_values[..., None] * attended
        mixed_heads = (
            jnp.einsum("btse,btsh->bteh", expert_hot, weighted, precision=HIGHEST)
            .reshape(seqs, local, experts * head)
            .astype(jnp.bfloat16)
        )
        hidden = inputs + jnp.dot(mixed_heads, out_mat, preferred_element_type=jnp.float32)
        normed_two, norm_pull_two = jax.vjp(normalize, hidden, gain_two_f)
        normed_two_low = normed_two.astype(jnp.bfloat16)
        pre_act = jnp.dot(normed_two_low, up_mat, preferred_element_type=jnp.float32)
        act_values, act_pull = jax.vjp(smooth_unit, pre_act)
        activated = act_values.astype(jnp.bfloat16)
        layer_parts.append(
            hidden + jnp.dot(activated, down_mat, preferred_element_type=jnp.float32)
        )
        totals[7] = totals[7] + jnp.einsum(
            "btf,btd->fd", activated, seq_cotangent, preferred_element_type=jnp.float32
        )
        back_act = jnp.einsum(
            "btd,fd->btf", seq_cotangent, down_mat, preferred_element_type=jnp.float32
        )
        (back_pre_f,) = act_pull(back_act)
        back_pre = back_pre_f.astype(jnp.bfloat16)
        totals[6] = totals[6] + jnp.einsum(
            "btd,btf->df", normed_two_low, back_pre, preferred_element_type=jnp.float32
        )
        back_normed_two = jnp.einsum(
            "btf,df->btd", back_pre, up_mat, preferred_element_type=jnp.float32
        )
        hidden_part, gain_two_grad = norm_pull_two(back_normed_two)
        back_hidden = seq_cotangent.astype(jnp.float32) + hidden_part
        totals[5] = totals[5] + gain_two_grad
        back_branch = back_hidden.astype(jnp.bfloat16)
        totals[4] = totals[4] + jnp.einsum(
            "btk,btd->kd", mixed_heads, back_branch, preferred_element_type=jnp.float32
        )
        back_mixed = jnp.einsum(
            "btd,kd->btk", back_branch, out_mat, preferred_element_type=jnp.float32
        ).reshape(seqs, local, experts, head)
        back_slots = jnp.einsum("btse,bteh->btsh", expert_hot, back_mixed, precision=HIGHEST)
        back_gates = jnp.sum(back_slots * attended, axis=-1)
        back_attended = (gate_values[..., None] * back_slots).astype(jnp.bfloat16)
        row_delta = jnp.sum(back_attended.astype(jnp.float32) * attended, axis=-1)
        (back_logits,) = gate_pull(back_gates)
        back_query, full_kv = key_range_grads(
            queries,
            back_attended,
            kv_all,
            query_places,
            key_places,
            log_total,
            row_delta,
            0,
            length,
        )
        own_kv = lax.psum_scatter(full_kv, "ctx", scatter_dimension=1, tiled=True)
        back_kv_low = own_kv.astype(jnp.bfloat16)
        back_query_low = back_query.astype(jnp.bfloat16)
        back_qall = (
            (
                jnp.einsum(
                    "btse,btsh->bteh",
                    expert_hot.astype(jnp.bfloat16),
                    back_query_low,
                    preferred_element_type=jnp.float32,
                )
                * 0.125
            )
            .reshape(seqs, local, experts * head)
            .astype(jnp.bfloat16)
        )
        totals[2] = totals[2] + jnp.einsum(
            "btd,btk->dk", normed_low, back_qall, preferred_element_type=jnp.float32
        )
        totals[3] = totals[3] + jnp.einsum(
            "btd,btk->dk", normed_low, back_kv_low, preferred_element_type=jnp.float32
        )
        totals[1] = totals[1] + jnp.einsum(
            "btd,bte->de", normed_low.astype(jnp.float32), back_logits, precision=HIGHEST
        )
        back_normed = jnp.einsum(
            "btk,dk->btd", back_qall, query_mat, preferred_element_type=jnp.float32
        )
        back_normed = back_normed + jnp.einsum(
            "btk,dk->btd", back_kv_low, kv_mat, preferred_element_type=jnp.float32
        )
        back_normed = back_normed + jnp.einsum(
            "bte,de->btd", back_logits, router_f, precision=HIGHEST
        )
        input_part, gain_one_grad = norm_pull_one(back_normed)
        totals[0] = totals[0] + gain_one_grad
        input_parts.append(back_hidden + input_part)
    layer_out = jnp.concatenate(layer_parts, axis=0)
    input_grad = jnp.concatenate(input_parts, axis=0)
    owned = (
        lax.psum_scatter(
            totals[0].astype(jnp.bfloat16), "wsh", scatter_dimension=0, tiled=True
        ).astype(jnp.float32),
        lax.psum_scatter(
            totals[1].astype(jnp.bfloat16), "wsh", scatter_dimension=0, tiled=True
        ).astype(jnp.float32),
        lax.psum_scatter(
            totals[2].astype(jnp.bfloat16), "wsh", scatter_dimension=0, tiled=True
        ).astype(jnp.float32),
        lax.psum_scatter(
            totals[3].astype(jnp.bfloat16), "wsh", scatter_dimension=0, tiled=True
        ).astype(jnp.float32),
        lax.psum_scatter(
            totals[4].astype(jnp.bfloat16), "wsh", scatter_dimension=0, tiled=True
        ).astype(jnp.float32),
        lax.psum_scatter(
            totals[5].astype(jnp.bfloat16), "wsh", scatter_dimension=0, tiled=True
        ).astype(jnp.float32),
        lax.psum_scatter(
            totals[6].astype(jnp.bfloat16), "wsh", scatter_dimension=0, tiled=True
        ).astype(jnp.float32),
        lax.psum_scatter(
            totals[7].astype(jnp.bfloat16), "wsh", scatter_dimension=0, tiled=True
        ).astype(jnp.float32),
    )
    summed = lax.psum(
        (owned[0], owned[1], owned[2], owned[3], owned[4], owned[5], owned[6], owned[7]), "ctx"
    )
    return (
        layer_out,
        input_grad,
        summed[0],
        summed[1],
        summed[2],
        summed[3],
        summed[4],
        summed[5],
        summed[6],
        summed[7],
    )


def solution(mesh):
    placed = (
        P("wsh", "ctx", None),
        P("wsh", "ctx", None),
        P(),
        P("wsh"),
        P("wsh", None),
        P("wsh", None),
        P("wsh", None),
        P("wsh", None),
        P("wsh"),
        P("wsh", None),
        P("wsh", None),
        P("wsh", "ctx", None),
    )
    return jax.shard_map(
        on_device,
        mesh=mesh,
        in_specs=placed,
        out_specs=(
            P("wsh", "ctx", None),
            P("wsh", "ctx", None),
            P("wsh"),
            P("wsh", None),
            P("wsh", None),
            P("wsh", None),
            P("wsh", None),
            P("wsh"),
            P("wsh", None),
            P("wsh", None),
        ),
        check_vma=False,
    )
```

profile of v0, /device:TPU:0, one launch (start us, length us, event | category | flops | bytes accessed | tf_op | source)
XLA Modules:
  0.0 953.8 jit_solution(5892758774405874934)
XLA Ops:
  8.8 1.9 all-gather.4
  12.8 1.8 all_gather.37
  17.8 1.9 all_gather.39
  20.5 2.6 all_gather.38
  30.5 45.1 %all-gather.3 = bf16[2048,128]{1,0:T(8,128)(2,1)S(1)} all-gather(bf16[128,128]{1,0:T(8,128)(2,1)S(1)} %convolution_convert_fusion.8), channel_id=5, replica_groups=mesh['ctx'=16,'wsh'=2] {'ctx'}, dimensions={0}, use_global_device_ids=true | all-gather | bytes 557056 | tf_op jit(solution)/shard_map/all_gather | solution.py:188
  75.7 38.7 %all-gather.2 = bf16[2048,128]{1,0:T(8,128)(2,1)S(1)} all-gather(bf16[128,128]{1,0:T(8,128)(2,1)S(1)} %convolution_convert_fusion.9), channel_id=4, replica_groups=mesh['ctx'=16,'wsh'=2] {'ctx'}, dimensions={0}, use_global_device_ids=true | all-gather | bytes 557056 | tf_op jit(solution)/shard_map/all_gather | solution.py:188
  114.3 40.8 %all-gather.1 = bf16[2048,128]{1,0:T(8,128)(2,1)S(1)} all-gather(bf16[128,128]{1,0:T(8,128)(2,1)S(1)} %convolution_convert_fusion.10), channel_id=3, replica_groups=mesh['ctx'=16,'wsh'=2] {'ctx'}, dimensions={0}, use_global_device_ids=true | all-gather | bytes 557056 | tf_op jit(solution)/shard_map/all_gather | solution.py:188
  155.1 2.4 all_gather.41
  167.1 3.2 broadcast_multiply_fusion.1
  171.9 2.6 convolution_convert_fusion.1
  176.3 2.5 broadcast_multiply_fusion.2
  184.3 2.0 all-gather.5
  189.0 5.5 multiply_convert_fusion
  194.6 3.2 add_convert_fusion.2
  198.8 3.7 multiply_convert_fusion.1
  202.5 4.2 multiply_convert_fusion.2
  214.2 1.9 copy.311
  216.1 2.4 fusion.191
  221.8 3.0 convolution_bitcast_fusion
  229.6 1.9 copy.304
  231.6 2.4 fusion.193
  235.5 2.1 multiply_reduce_fusion.7
  239.4 1.9 fusion.137
  241.3 1.9 copy.297
  243.2 2.4 fusion.195
  247.2 2.3 pad_maximum_fusion.4
  252.6 2.6 fusion.5
  258.8 2.7 fusion.6
  267.7 2.4 fusion.17
  270.2 2.2 fusion.15
  272.4 2.3 fusion.16
  282.7 1.8 copy.309
  294.7 1.8 fusion.317
  296.5 1.9 fusion.316
  298.4 1.9 fusion.311
  301.2 3.5 fusion.286
  304.7 2.8 fusion.282
  307.5 15.8 %reduce-scatter.17.cloned.1.call-done = f32[1,128,128]{1,2,0:T(8,128)} async-done(((f32[1,2048,128]{1,2,0:T(8,128)}), f32[1,128,128]{1,2,0:T(8,128)}) %reduce-scatter.17.cloned.1.call-update) | async-done | bytes 65552 | tf_op jit(solution)/shard_map/reduce_scatter | solution.py:246
  323.3 2.0 fusion.18
  325.3 75.0 %reduce-scatter.15.cloned.1.call-done = f32[1,128,128]{1,2,0:T(8,128)} async-done(((f32[1,2048,128]{1,2,0:T(8,128)}), f32[1,128,128]{1,2,0:T(8,128)}) %reduce-scatter.15.cloned.1.call-update) | async-done | bytes 65552 | tf_op jit(solution)/shard_map/reduce_scatter | solution.py:246
  400.3 2.0 fusion.19
  402.3 75.0 %reduce-scatter.13.cloned.1.call-done = f32[1,128,128]{1,2,0:T(8,128)} async-done(((f32[1,2048,128]{1,2,0:T(8,128)}), f32[1,128,128]{1,2,0:T(8,128)}) %reduce-scatter.13.cloned.1.call-update) | async-done | bytes 65552 | tf_op jit(solution)/shard_map/reduce_scatter | solution.py:246
  477.3 3.0 fusion.99
  489.3 1.9 fusion.180
  491.2 1.9 copy.263
  493.1 2.4 fusion.198
  497.1 39.5 %all-gather = bf16[2048,128]{1,0:T(8,128)(2,1)S(1)} all-gather(bf16[128,128]{1,0:T(8,128)(2,1)} %convolution_convert_fusion.11), channel_id=2, replica_groups=mesh['ctx'=16,'wsh'=2] {'ctx'}, dimensions={0}, use_global_device_ids=true | all-gather | bytes 557056 | tf_op jit(solution)/shard_map/all_gather | solution.py:188
  541.7 2.6 convolution_convert_fusion.3
  544.3 1.8 copy.268
  547.6 5.0 multiply_convert_fusion.3
  557.7 1.9 copy.290
  559.6 2.4 fusion.197
  564.7 2.2 convolution_bitcast_fusion.6
  582.4 2.3 fusion.14
  589.3 3.8 fusion.290
  593.2 53.5 %reduce-scatter.11.cloned.1.call-done = f32[1,128,128]{1,2,0:T(8,128)} async-done(((f32[1,2048,128]{1,2,0:T(8,128)}), f32[1,128,128]{1,2,0:T(8,128)}) %reduce-scatter.11.cloned.1.call-update) | async-done | bytes 65552 | tf_op jit(solution)/shard_map/reduce_scatter | solution.py:246
  651.8 7.0 add_convert_fusion.1
  660.7 2.3 fusion.29
  668.0 2.1 add_convert_fusion
  678.4 2.5 all-reduce.3
  683.6 3.4 reduce-scatter.23.cloned.1.call-done
  687.0 13.6 %reduce-scatter.27.cloned.1.call-done = bf16[256,2048]{1,0:T(8,128)(2,1)} async-done(((bf16[512,2048]{1,0:T(8,128)(2,1)}), bf16[256,2048]{1,0:T(8,128)(2,1)}) %reduce-scatter.27.cloned.1.call-update) | async-done | bytes 1048592 | tf_op jit(solution)/shard_map/reduce_scatter | solution.py:304
  700.7 13.6 %reduce-scatter.29.cloned.1.call-done = bf16[1024,512]{1,0:T(8,128)(2,1)} async-done(((bf16[2048,512]{1,0:T(8,128)(2,1)}), bf16[1024,512]{1,0:T(8,128)(2,1)}) %reduce-scatter.29.cloned.1.call-update) | async-done | bytes 1048592 | tf_op jit(solution)/shard_map/reduce_scatter | solution.py:307
  714.2 232.3 %all-reduce.5 = (f32[256]{0:T(256)}, f32[256,8]{0,1:T(8,128)}, f32[256,512]{1,0:T(8,128)}, f32[256,128]{1,0:T(8,128)}, f32[256,512]{1,0:T(8,128)}, /*index=5*/f3...) all-reduce(f32[256]{0:T(256)S(1)} %dynamic-slice_convert_fusion.1, ...), channel_id=1, replica_groups=mesh['ctx'=16,'wsh'=2] {'ctx'}, use_global_device_ids=true, to_apply=%region_77.78 | all-reduce | flops 1346048 | bytes 8077312 | tf_op jit(solution)/shard_map/psum | solution.py:311
  (671 shorter events, 155.0 us)
Async XLA Ops:
  7.2 10.6 %copy-start.102 = (bf16[256,128]{1,0:T(8,128)(2,1)S(1)}, bf16[256,128]{1,0:T(8,128)(2,1)}, u32[]{:S(2)}) copy-start(bf16[256,128]{1,0:T(8,128)(2,1)} %param.18) | copy-start | bytes 196612
  7.2 181.7 %all-gather.9.cloned.1.call-start = ((), (), s32[]{:S(2)}) async-start(), calls=%async_computation.10 | async-start | bytes 3145728 | tf_op jit(solution)/shard_map/all_gather | solution.py:145
  8.0 12.4 %copy-start.98 = (bf16[256,512]{1,0:T(8,128)(2,1)S(1)}, bf16[256,512]{1,0:T(8,128)(2,1)}, u32[]{:S(2)}) copy-start(bf16[256,512]{1,0:T(8,128)(2,1)} %param.17) | copy-start | bytes 786436
  8.0 186.6 %all-gather.11.cloned.1.call-start = ((), (), s32[]{:S(2)}) async-start(), calls=%async_computation.11 | async-start | bytes 3145728 | tf_op jit(solution)/shard_map/all_gather | solution.py:146
  8.7 314.6 %reduce-scatter.17.cloned.1.call-start = ((), (), s32[]{:S(2)}) async-start(), calls=%async_computation.15 | async-start | bytes 1114112 | tf_op jit(solution)/shard_map/reduce_scatter | solution.py:246
  10.9 9.2 copy-start.131
  11.7 11.7 %copy-start.180 = (f32[128]{0:T(128)}, f32[128]{0:T(128)S(1)}, u32[]{:S(2)}) copy-start(f32[128]{0:T(128)S(1)} %fusion.249) | copy-start | bytes 1540
  12.1 11.3 %copy-start.136 = (f32[128]{0:T(128)}, f32[128]{0:T(128)S(1)}, u32[]{:S(2)}) copy-start(f32[128]{0:T(128)S(1)} %fusion.251) | copy-start | bytes 1540
  12.2 11.2 %copy-start.183 = (f32[128]{0:T(128)}, f32[128]{0:T(128)S(1)}, u32[]{:S(2)}) copy-start(f32[128]{0:T(128)S(1)} %fusion.253) | copy-start | bytes 1540
  12.8 10.6 %copy-start.119 = (s32[128,2]{0,1:T(2,128)}, s32[128,2]{0,1:T(2,128)S(1)}, u32[]{:S(2)}) copy-start(s32[128,2]{0,1:T(2,128)S(1)} %get-tuple-element.384) | copy-start | bytes 3076
  12.8 11.8 %copy-start.118 = (s32[128,2]{0,1:T(2,128)}, s32[128,2]{0,1:T(2,128)S(1)}, u32[]{:S(2)}) copy-start(s32[128,2]{0,1:T(2,128)S(1)} %get-tuple-element.385) | copy-start | bytes 3076
  14.8 11.8 %copy-start.104 = (s32[128,2]{1,0:T(8,128)}, s32[128,2]{1,0:T(8,128)S(1)}, u32[]{:S(2)}) copy-start(s32[128,2]{1,0:T(8,128)S(1)} %copy.269) | copy-start | bytes 3076
  15.0 8.8 copy-start.28
  15.0 8.8 copy-start.32
  15.0 8.8 copy-start.34
  15.2 8.6 copy-start.111
  15.2 9.5 copy-start.161
  16.4 11.2 %copy-start.105 = (s32[128,2]{1,0:T(8,128)}, s32[128,2]{1,0:T(8,128)S(1)}, u32[]{:S(2)}) copy-start(s32[128,2]{1,0:T(8,128)S(1)} %copy.276) | copy-start | bytes 3076
  27.3 130.2 %copy-start.91 = (f32[128,2,64]{0,2,1:T(8,128)}, f32[128,2,64]{0,2,1:T(8,128)S(1)}, u32[]{:S(2)}) copy-start(f32[128,2,64]{0,2,1:T(8,128)S(1)} %copy.271) | copy-start | bytes 196612
  28.2 126.9 %copy-start.95 = (bf16[256,512]{1,0:T(8,128)(2,1)S(1)}, bf16[256,512]{1,0:T(8,128)(2,1)}, u32[]{:S(2)}) copy-start(bf16[256,512]{1,0:T(8,128)(2,1)} %param.19) | copy-start | bytes 786436
  75.7 86.4 %copy-start.44 = (bf16[2048,128]{1,0:T(8,128)(2,1)}, bf16[2048,128]{1,0:T(8,128)(2,1)S(1)}, u32[]{:S(2)}) copy-start(bf16[2048,128]{1,0:T(8,128)(2,1)S(1)} %all-gather.3) | copy-start | bytes 1572868
  114.3 44.3 %copy-start.40 = (bf16[2048,128]{1,0:T(8,128)(2,1)}, bf16[2048,128]{1,0:T(8,128)(2,1)S(1)}, u32[]{:S(2)}) copy-start(bf16[2048,128]{1,0:T(8,128)(2,1)S(1)} %all-gather.2) | copy-start | bytes 1572868
  114.3 43.8 %copy-start.93 = (f32[128,2,64]{0,2,1:T(8,128)S(1)}, f32[128,2,64]{0,2,1:T(8,128)}, u32[]{:S(2)}) copy-start(f32[128,2,64]{0,2,1:T(8,128)} %copy.285) | copy-start | bytes 196612
  167.1 9.2 copy-start.6
  167.1 9.2 copy-start.168
  183.1 11.4 %copy-start.18 = (f32[1,128,512]{2,1,0:T(8,128)}, f32[1,128,512]{2,1,0:T(8,128)S(1)}, u32[]{:S(2)}) copy-start(f32[1,128,512]{2,1,0:T(8,128)S(1)} %get-tuple-element.413) | copy-start | bytes 786436
  183.5 15.2 %copy-start.22 = (f32[1,128,512]{2,1,0:T(8,128)}, f32[1,128,512]{2,1,0:T(8,128)S(1)}, u32[]{:S(2)}) copy-start(f32[1,128,512]{2,1,0:T(8,128)S(1)} %get-tuple-element.408) | copy-start | bytes 786436
  183.5 15.2 %copy-start.145 = (f32[128]{0:T(128)}, f32[128]{0:T(128)S(1)}, u32[]{:S(2)}) copy-start(f32[128]{0:T(128)S(1)} %broadcast_multiply_fusion.7) | copy-start | bytes 1540
  183.9 10.6 %copy-start.15 = (f32[1,128,512]{2,1,0:T(8,128)}, f32[1,128,512]{2,1,0:T(8,128)S(1)}, u32[]{:S(2)}) copy-start(f32[1,128,512]{2,1,0:T(8,128)S(1)} %get-tuple-element.403) | copy-start | bytes 786436
  183.9 10.6 %copy-start.138 = (f32[128]{0:T(128)}, f32[128]{0:T(128)S(1)}, u32[]{:S(2)}) copy-start(f32[128]{0:T(128)S(1)} %broadcast_multiply_fusion.5) | copy-start | bytes 1540
  184.1 10.4 %copy-start.202 = (f32[128]{0:T(128)}, f32[128]{0:T(128)S(1)}, u32[]{:S(2)}) copy-start(f32[128]{0:T(128)S(1)} %multiply_reduce_fusion.2) | copy-start | bytes 1540
  184.3 10.2 %copy-start.200 = (f32[128]{0:T(128)}, f32[128]{0:T(128)S(1)}, u32[]{:S(2)}) copy-start(f32[128]{0:T(128)S(1)} %multiply_reduce_fusion.1) | copy-start | bytes 1540
  187.3 7.3 copy-start.204
  188.9 9.8 %copy-start.155 = (f32[128]{0:T(128)}, f32[128]{0:T(128)S(1)}, u32[]{:S(2)}) copy-start(f32[128]{0:T(128)S(1)} %fusion.252) | copy-start | bytes 1540
  249.5 150.9 %reduce-scatter.15.cloned.1.call-start = ((), (), s32[]{:S(2)}) async-start(), calls=%async_computation.14 | async-start | bytes 1114112 | tf_op jit(solution)/shard_map/reduce_scatter | solution.py:246
  265.1 9.5 copy-start.51
  265.1 9.5 copy-start.90
  267.7 7.2 copy-start.9
  267.7 7.2 copy-start.101
  267.7 7.3 copy-start.169
  276.7 200.6 %reduce-scatter.13.cloned.1.call-start = ((), (), s32[]{:S(2)}) async-start(), calls=%async_computation.13 | async-start | bytes 1114112 | tf_op jit(solution)/shard_map/reduce_scatter | solution.py:246
  284.4 7.8 copy-start.7
  284.4 7.8 copy-start.100
  294.6 352.0 %reduce-scatter.11.cloned.1.call-start = ((), (), s32[]{:S(2)}) async-start(), calls=%async_computation.12 | async-start | bytes 1114112 | tf_op jit(solution)/shard_map/reduce_scatter | solution.py:246
  547.4 8.3 copy-start.26
  547.4 8.3 copy-start.148
  547.6 8.1 copy-start.159
  559.6 7.3 copy-start.47
  570.1 7.9 copy-start.53
  571.8 103.9 %reduce-scatter.19.cloned.1.call-start = ((), (), s32[]{:S(2)}) async-start(), calls=%async_computation.16 | async-start | bytes 12288 | tf_op jit(solution)/shard_map/reduce_scatter | solution.py:289
  582.1 93.6 %reduce-scatter.25.cloned.1.call-start = ((), (), s32[]{:S(2)}) async-start(), calls=%async_computation.19 | async-start | bytes 786432 | tf_op jit(solution)/shard_map/reduce_scatter | solution.py:298
  585.8 90.5 %reduce-scatter.21.cloned.1.call-start = ((), (), s32[]{:S(2)}) async-start(), calls=%async_computation.17 | async-start | bytes 786432 | tf_op jit(solution)/shard_map/reduce_scatter | solution.py:292
  589.2 97.8 %reduce-scatter.23.cloned.1.call-start = ((), (), s32[]{:S(2)}) async-start(), calls=%async_computation.18 | async-start | bytes 196608 | tf_op jit(solution)/shard_map/reduce_scatter | solution.py:295
  593.2 58.6 %copy-start.17 = (f32[1,128,512]{2,1,0:T(8,128)S(1)}, f32[1,128,512]{2,1,0:T(8,128)}, u32[]{:S(2)}) copy-start(f32[1,128,512]{2,1,0:T(8,128)} %copy-done.15) | copy-start | bytes 786436
  651.7 48.9 %reduce-scatter.27.cloned.1.call-start = ((), (), s32[]{:S(2)}) async-start(), calls=%async_computation.20 | async-start | bytes 3145728 | tf_op jit(solution)/shard_map/reduce_scatter | solution.py:304
  658.8 55.4 %reduce-scatter.29.cloned.1.call-start = ((), (), s32[]{:S(2)}) async-start(), calls=%async_computation.21 | async-start | bytes 3145728 | tf_op jit(solution)/shard_map/reduce_scatter | solution.py:307
  673.0 8.1 copy-start.39
  673.0 8.1 copy-start.58
  673.0 8.1 copy-start.60
  673.1 8.0 copy-start.185
  673.7 7.4 copy-start.199
  682.2 32.0 %copy-start.96 = (bf16[256,512]{1,0:T(8,128)(2,1)S(1)}, bf16[256,512]{1,0:T(8,128)(2,1)}, u32[]{:S(2)}) copy-start(bf16[256,512]{1,0:T(8,128)(2,1)} %reduce-scatter.25.cloned.1.call-done) | copy-start | bytes 786436
  682.2 32.0 %copy-start.97 = (bf16[256,512]{1,0:T(8,128)(2,1)S(1)}, bf16[256,512]{1,0:T(8,128)(2,1)}, u32[]{:S(2)}) copy-start(bf16[256,512]{1,0:T(8,128)(2,1)} %reduce-scatter.21.cloned.1.call-done) | copy-start | bytes 786436
  682.2 32.0 %copy-start.167 = (bf16[256,8]{0,1:T(8,128)(2,1)S(1)}, bf16[256,8]{0,1:T(8,128)(2,1)}, u32[]{:S(2)}) copy-start(bf16[256,8]{0,1:T(8,128)(2,1)} %reduce-scatter.19.cloned.1.call-done) | copy-start | bytes 12292
  (159 other events, 460.9 us)
Sparse Core Ops, SparseCore 0:
  9.6 13.6 all-gather.8
  24.8 11.3 all-gather.10
  249.6 73.6 reduce-scatter.16
  326.1 74.1 reduce-scatter.14
  403.0 74.2 reduce-scatter.12
  571.9 74.7 reduce-scatter.10
  649.4 3.9 reduce-scatter.18
  655.6 9.1 reduce-scatter.24
  667.2 9.0 reduce-scatter.20
  678.4 8.6 reduce-scatter.22
  689.9 10.7 reduce-scatter.26
  703.4 10.7 reduce-scatter.28
where the time goes:
time: 961 us; the launch traced here: 954 us
  blocking collectives  411 us (43%)
  waiting for transfers between devices  252 us (26%)
  matrix products  171 us (18%)
  local copies, waits for them, and re-layouts  55.3 us (6%)
  other arithmetic  44.9 us (5%)
  between operations  18.1 us (2%)
    psum x1, blocking collectives, on_device(): lax.psum((owned[0], owned[1], owned[2], owned[3], owned[4], owned[5], own...  232 us
    reduce_scatter x4, waiting for transfers between devices, on_device(): own_kv = lax.psum_scatter(full_kv, 'ctx', scatter_dimension=1, tiled=True)  219 us
    all_gather x4, blocking collectives, on_device(): kv_all = lax.all_gather(keyval, 'ctx', axis=1, tiled=True)  164 us
  transfers between devices with their start and end apart: 12, of which 8 were waited for; matrix products, arithmetic and copies ran while one was open for 16% of the time, Pallas kernels for 0%

commit v1 on v0

--- a/solution.py
+++ b/solution.py
@@ -185,7 +185,15 @@
         keyval = jnp.dot(normed_low, kv_mat, preferred_element_type=jnp.float32).astype(
             jnp.bfloat16
         )
-        kv_all = lax.all_gather(keyval, "ctx", axis=1, tiled=True)
+        ways, here = (lax.axis_size("ctx"), lax.axis_index("ctx"))
+        grown, reach = (keyval, 1)
+        while reach < ways:
+            theirs = lax.ppermute(grown, "ctx", [(d, d ^ reach) for d in range(ways)])
+            mine_first = jnp.concatenate([grown, theirs], axis=1)
+            theirs_first = jnp.concatenate([theirs, grown], axis=1)
+            grown = jnp.where(here & reach == 0, mine_first, theirs_first)
+            reach = 2 * reach
+        kv_all = grown
         log_total = log_totals(queries, kv_all, query_places, key_places)
         attended = attend(queries, kv_all, query_places, key_places, log_total)
         weighted = gate_values[..., None] * attended

time: 961 us -> 874 us (0.909)
  blocking collectives: 411 us -> 247 us
  waiting for transfers between devices: 252 us -> 295 us
  other arithmetic: 44.9 us -> 63.3 us
  starting transfers between devices: 0.92 us -> 18.4 us
    all_gather x4 -> x0, blocking collectives: 164 us -> none  [on_device(): kv_all = lax.all_gather(keyval, 'ctx', axis=1, tiled=True)]
    ppermute x0 -> x16, waiting for transfers between devices: none -> 43 us  [on_device(): theirs = lax.ppermute(grown, 'ctx', [(d, d ^ reach) for d in range(ways)])]
    ppermute x0 -> x16, starting transfers between devices: none -> 17.3 us  [on_device(): theirs = lax.ppermute(grown, 'ctx', [(d, d ^ reach) for d in range(ways)])]
  transfers between devices with their start and end apart: 12 -> 28, of which waited for: 8 -> 15; matrix products, arithmetic and copies ran while one was open for 16% -> 21% of each run, Pallas kernels for 0% -> 0%
where the time goes in v1:
time: 874 us; the launch traced here: 866 us
  waiting for transfers between devices  295 us (34%)
  blocking collectives  247 us (28%)
  matrix products  170 us (19%)
  other arithmetic  63.3 us (7%)
  local copies, waits for them, and re-layouts  54.5 us (6%)
  starting transfers between devices  18.4 us (2%)
  between operations  18.1 us (2%)
    psum x1, blocking collectives, on_device(): lax.psum((owned[0], owned[1], owned[2], owned[3], owned[4], owned[5], own...  232 us
    reduce_scatter x4, waiting for transfers between devices, on_device(): own_kv = lax.psum_scatter(full_kv, 'ctx', scatter_dimension=1, tiled=True)  224 us
    ppermute x16, waiting for transfers between devices, on_device(): theirs = lax.ppermute(grown, 'ctx', [(d, d ^ reach) for d in range(ways)])  43 us
    dot_general x4, matrix products, on_device(): jnp.dot(normed_two_low, up_mat, preferred_element_type=jnp.float32)  18.4 us
  transfers between devices with their start and end apart: 28, of which 15 were waited for; matrix products, arithmetic and copies ran while one was open for 21% of the time, Pallas kernels for 0%

profile of v1, /device:TPU:0, one launch (start us, length us, event | category | flops | bytes accessed | tf_op | source)
XLA Modules:
  0.0 865.8 jit_solution(11327016094311856697)
XLA Ops:
  9.9 2.0 all-gather
  11.9 2.1 all_gather.27
  16.4 2.9 collective-permute-start.12
  19.7 2.1 collective-permute-start.4
  29.6 2.2 all_gather.26
  37.3 2.2 all_gather.28
  40.2 2.0 all-gather.1
  57.9 2.7 collective-permute-start.15
  60.5 6.4 collective-permute-done.6
  68.4 1.8 collective-permute-start.11
  70.4 20.1 %collective-permute-done.7 = bf16[1,1024,128]{2,1,0:T(8,128)(2,1)S(1)} collective-permute-done((bf16[1,1024,128]{2,1,0:T(8,128)(2,1)S(1)}, bf16[1,1024,128]{2,1,0:T(8,128)(2,1)S(1)}, u32[]{:S(2)}, u32[]{:S(2)}) %collective-permute-start.7) | collective-permute-done | bytes 262176 | tf_op jit(solution)/shard_map/ppermute | solution.py:191
  99.7 2.5 convolution_convert_fusion
  102.2 3.2 broadcast_multiply_fusion.1
  107.0 2.6 convolution_convert_fusion.1
  111.3 2.5 broadcast_multiply_fusion.2
  120.3 5.9 multiply_convert_fusion
  126.3 3.2 add_convert_fusion.2
  130.5 3.7 multiply_convert_fusion.1
  134.2 3.7 multiply_convert_fusion.2
  145.5 1.9 copy.311
  147.4 2.4 fusion.195
  153.0 3.0 convolution_bitcast_fusion
  160.8 1.9 copy.304
  162.8 2.3 fusion.197
  166.7 2.1 multiply_reduce_fusion.7
  170.6 1.9 fusion.141
  172.5 1.9 copy.297
  174.4 2.4 fusion.199
  178.4 2.3 pad_maximum_fusion.4
  183.9 2.6 fusion.5
  190.1 2.7 fusion.6
  199.0 2.4 fusion.17
  201.4 2.3 fusion.15
  203.7 2.3 fusion.16
  227.9 1.9 fusion.320
  229.8 1.9 fusion.315
  232.7 3.5 fusion.290
  236.2 2.8 fusion.286
  239.0 19.0 %reduce-scatter.17.cloned.1.call-done = f32[1,128,128]{1,2,0:T(8,128)} async-done(((f32[1,2048,128]{1,2,0:T(8,128)}), f32[1,128,128]{1,2,0:T(8,128)}) %reduce-scatter.17.cloned.1.call-update) | async-done | bytes 65552 | tf_op jit(solution)/shard_map/reduce_scatter | solution.py:254
  257.9 2.0 fusion.18
  259.9 75.0 %reduce-scatter.15.cloned.1.call-done = f32[1,128,128]{1,2,0:T(8,128)} async-done(((f32[1,2048,128]{1,2,0:T(8,128)}), f32[1,128,128]{1,2,0:T(8,128)}) %reduce-scatter.15.cloned.1.call-update) | async-done | bytes 65552 | tf_op jit(solution)/shard_map/reduce_scatter | solution.py:254
  334.9 2.0 fusion.19
  336.9 74.9 %reduce-scatter.13.cloned.1.call-done = f32[1,128,128]{1,2,0:T(8,128)} async-done(((f32[1,2048,128]{1,2,0:T(8,128)}), f32[1,128,128]{1,2,0:T(8,128)}) %reduce-scatter.13.cloned.1.call-update) | async-done | bytes 65552 | tf_op jit(solution)/shard_map/reduce_scatter | solution.py:254
  411.7 3.0 fusion.99
  420.7 1.9 copy.263
  422.7 2.4 fusion.202
  427.6 3.4 collective-permute-done.1
  440.4 7.8 collective-permute-done.3
  452.6 2.6 convolution_convert_fusion.3
  458.5 5.0 multiply_convert_fusion.3
  468.6 1.9 copy.290
  470.5 2.7 fusion.201
  475.9 2.2 convolution_bitcast_fusion.6
  493.3 2.3 fusion.14
  500.2 3.8 fusion.294
  504.1 54.7 %reduce-scatter.11.cloned.1.call-done = f32[1,128,128]{1,2,0:T(8,128)} async-done(((f32[1,2048,128]{1,2,0:T(8,128)}), f32[1,128,128]{1,2,0:T(8,128)}) %reduce-scatter.11.cloned.1.call-update) | async-done | bytes 65552 | tf_op jit(solution)/shard_map/reduce_scatter | solution.py:254
  563.9 7.0 add_convert_fusion.1
  572.8 2.3 fusion.29
  580.5 2.1 add_convert_fusion
  588.8 2.0 fusion.89
  592.5 2.6 all-reduce.3
  599.1 13.5 %reduce-scatter.27.cloned.1.call-done = bf16[256,2048]{1,0:T(8,128)(2,1)} async-done(((bf16[512,2048]{1,0:T(8,128)(2,1)}), bf16[256,2048]{1,0:T(8,128)(2,1)}) %reduce-scatter.27.cloned.1.call-update) | async-done | bytes 1048592 | tf_op jit(solution)/shard_map/reduce_scatter | solution.py:312
  612.6 13.6 %reduce-scatter.29.cloned.1.call-done = bf16[1024,512]{1,0:T(8,128)(2,1)} async-done(((bf16[2048,512]{1,0:T(8,128)(2,1)}), bf16[1024,512]{1,0:T(8,128)(2,1)}) %reduce-scatter.29.cloned.1.call-update) | async-done | bytes 1048592 | tf_op jit(solution)/shard_map/reduce_scatter | solution.py:315
  626.2 232.2 %all-reduce.5 = (f32[256]{0:T(256)}, f32[256,8]{0,1:T(8,128)}, f32[256,512]{1,0:T(8,128)}, f32[256,128]{1,0:T(8,128)}, f32[256,512]{1,0:T(8,128)}, /*index=5*/f3...) all-reduce(f32[256]{0:T(256)S(1)} %dynamic-slice_convert_fusion.1, ...), channel_id=1, replica_groups=mesh['ctx'=16,'wsh'=2] {'ctx'}, use_global_device_ids=true, to_apply=%region_77.78 | all-reduce | flops 1346048 | bytes 8077312 | tf_op jit(solution)/shard_map/psum | solution.py:319
  (691 shorter events, 187.7 us)
Async XLA Ops:
  7.2 8.8 %copy-start.12 = (bf16[4,128,512]{2,1,0:T(8,128)(2,1)S(1)}, bf16[4,128,512]{2,1,0:T(8,128)(2,1)}, u32[]{:S(2)}) copy-start(bf16[4,128,512]{2,1,0:T(8,128)(2,1)} %param.12) | copy-start | bytes 1572868
  7.2 113.1 %all-gather.5.cloned.1.call-start = ((), (), s32[]{:S(2)}) async-start(), calls=%async_computation.10 | async-start | bytes 3145728 | tf_op jit(solution)/shard_map/all_gather | solution.py:145
  7.9 14.0 %copy-start.168 = (s32[4,128,2]{1,2,0:T(2,128)S(1)}, s32[4,128,2]{1,2,0:T(2,128)}, u32[]{:S(2)}) copy-start(s32[4,128,2]{1,2,0:T(2,128)} %param.13) | copy-start | bytes 12292
  7.9 14.5 %copy-start.167 = (bf16[256,8]{0,1:T(8,128)(2,1)S(1)}, bf16[256,8]{0,1:T(8,128)(2,1)}, u32[]{:S(2)}) copy-start(bf16[256,8]{0,1:T(8,128)(2,1)} %param.16) | copy-start | bytes 12292
  7.9 118.4 %all-gather.7.cloned.1.call-start = ((), (), s32[]{:S(2)}) async-start(), calls=%async_computation.11 | async-start | bytes 3145728 | tf_op jit(solution)/shard_map/all_gather | solution.py:146
  9.2 15.2 %copy-start.130 = (f32[128]{0:T(128)}, f32[128]{0:T(128)S(1)}, u32[]{:S(2)}) copy-start(f32[128]{0:T(128)S(1)} %broadcast_multiply_fusion.10) | copy-start | bytes 1540
  9.9 19.6 %copy-start.102 = (bf16[256,512]{1,0:T(8,128)(2,1)S(1)}, bf16[256,512]{1,0:T(8,128)(2,1)}, u32[]{:S(2)}) copy-start(bf16[256,512]{1,0:T(8,128)(2,1)} %param.17) | copy-start | bytes 786436
  15.4 16.4 %copy-start.179 = (f32[128]{0:T(128)}, f32[128]{0:T(128)S(1)}, u32[]{:S(2)}) copy-start(f32[128]{0:T(128)S(1)} %get-tuple-element.268) | copy-start | bytes 1540
  15.9 8.6 copy-start.173
  16.0 8.3 copy-start.133
  16.0 15.8 %copy-start.175 = (f32[128]{0:T(128)}, f32[128]{0:T(128)S(1)}, u32[]{:S(2)}) copy-start(f32[128]{0:T(128)S(1)} %fusion.257) | copy-start | bytes 1540
  16.2 15.9 %copy-start.32 = (bf16[1,128,512]{2,1,0:T(8,128)(2,1)}, bf16[1,128,512]{2,1,0:T(8,128)(2,1)S(1)}, u32[]{:S(2)}) copy-start(bf16[1,128,512]{2,1,0:T(8,128)(2,1)S(1)} %get-tuple-element.368) | copy-start | bytes 393220
  16.2 15.9 %copy-start.34 = (bf16[1,128,512]{2,1,0:T(8,128)(2,1)}, bf16[1,128,512]{2,1,0:T(8,128)(2,1)S(1)}, u32[]{:S(2)}) copy-start(bf16[1,128,512]{2,1,0:T(8,128)(2,1)S(1)} %get-tuple-element.367) | copy-start | bytes 393220
  16.2 16.2 %copy-start.28 = (bf16[1,128,512]{2,1,0:T(8,128)(2,1)}, bf16[1,128,512]{2,1,0:T(8,128)(2,1)S(1)}, u32[]{:S(2)}) copy-start(bf16[1,128,512]{2,1,0:T(8,128)(2,1)S(1)} %get-tuple-element.369) | copy-start | bytes 393220
  16.4 30.4 %collective-permute-start.12 = (bf16[1,128,128]{2,1,0:T(8,128)(2,1)S(1)}, bf16[1,128,128]{2,1,0:T(8,128)(2,1)S(1)}, u32[]{:S(2)}, u32[]{:S(2)}) collective-permute-start(bf16[1,128,128]{2,1,0:T(8,128)(2,1)S(1)} %bitcast.578), channel_id=1, source_target_pairs={{0,2},{2,0},{4,6},{6,4},{8,10},{10,8},{12,14},{14,12},{16,18},{18,... | collective-permute-start | bytes 98312 | tf_op jit(solution)/shard_map/ppermute | solution.py:191
  19.5 26.5 %collective-permute-start.8 = (bf16[1,128,128]{2,1,0:T(8,128)(2,1)S(1)}, bf16[1,128,128]{2,1,0:T(8,128)(2,1)}, u32[]{:S(2)}, u32[]{:S(2)}) collective-permute-start(bf16[1,128,128]{2,1,0:T(8,128)(2,1)S(1)} %bitcast.582), channel_id=1, source_target_pairs={{0,2},{2,0},{4,6},{6,4},{8,10},{10,8},{12,14},{14,12},{16,18},{18,... | collective-permute-start | bytes 98312 | tf_op jit(solution)/shard_map/ppermute | solution.py:191
  19.7 25.4 %collective-permute-start.4 = (bf16[1,128,128]{2,1,0:T(8,128)(2,1)S(1)}, bf16[1,128,128]{2,1,0:T(8,128)(2,1)}, u32[]{:S(2)}, u32[]{:S(2)}) collective-permute-start(bf16[1,128,128]{2,1,0:T(8,128)(2,1)S(1)} %bitcast.580), channel_id=1, source_target_pairs={{0,2},{2,0},{4,6},{6,4},{8,10},{10,8},{12,14},{14,12},{16,18},{18,... | collective-permute-start | bytes 98312 | tf_op jit(solution)/shard_map/ppermute | solution.py:191
  21.8 236.1 %reduce-scatter.17.cloned.1.call-start = ((), (), s32[]{:S(2)}) async-start(), calls=%async_computation.15 | async-start | bytes 1114112 | tf_op jit(solution)/shard_map/reduce_scatter | solution.py:254
  22.5 10.2 %copy-start.118 = (s32[128,2]{0,1:T(2,128)}, s32[128,2]{0,1:T(2,128)S(1)}, u32[]{:S(2)}) copy-start(s32[128,2]{0,1:T(2,128)S(1)} %get-tuple-element.385) | copy-start | bytes 3076
  22.5 10.3 %copy-start.120 = (s32[128,2]{0,1:T(2,128)}, s32[128,2]{0,1:T(2,128)S(1)}, u32[]{:S(2)}) copy-start(s32[128,2]{0,1:T(2,128)S(1)} %get-tuple-element.386) | copy-start | bytes 3076
  24.4 10.2 %copy-start.107 = (s32[128,2]{1,0:T(8,128)}, s32[128,2]{1,0:T(8,128)S(1)}, u32[]{:S(2)}) copy-start(s32[128,2]{1,0:T(8,128)S(1)} %copy.269) | copy-start | bytes 3076
  26.1 9.1 %copy-start.108 = (s32[128,2]{1,0:T(8,128)}, s32[128,2]{1,0:T(8,128)S(1)}, u32[]{:S(2)}) copy-start(s32[128,2]{1,0:T(8,128)S(1)} %copy.276) | copy-start | bytes 3076
  43.7 47.0 %copy-start.92 = (f32[128,2,64]{0,2,1:T(8,128)}, f32[128,2,64]{0,2,1:T(8,128)S(1)}, u32[]{:S(2)}) copy-start(f32[128,2,64]{0,2,1:T(8,128)S(1)} %copy.271) | copy-start | bytes 196612
  46.9 5.5 collective-permute-start.13
  49.3 7.5 collective-permute-start.9
  50.7 4.3 collective-permute-start.5
  52.4 5.3 collective-permute-start.14
  55.2 11.8 %collective-permute-start.6 = (bf16[1,512,128]{2,1,0:T(8,128)(2,1)S(1)}, bf16[1,512,128]{2,1,0:T(8,128)(2,1)S(1)}, u32[]{:S(2)}, u32[]{:S(2)}) collective-permute-start(bf16[1,512,128]{2,1,0:T(8,128)(2,1)S(1)} %maximum_select_fusion.15), channel_id=1, source_target_pairs={{0,8},{2,10},{4,12},{6,14},{8,0},{10,2},{12,4},{14,6},{16,24},{18,... | collective-permute-start | bytes 393224 | tf_op jit(solution)/shard_map/ppermute | solution.py:191
  56.9 11.4 %collective-permute-start.10 = (bf16[1,512,128]{2,1,0:T(8,128)(2,1)S(1)}, bf16[1,512,128]{2,1,0:T(8,128)(2,1)S(1)}, u32[]{:S(2)}, u32[]{:S(2)}) collective-permute-start(bf16[1,512,128]{2,1,0:T(8,128)(2,1)S(1)} %maximum_select_fusion.17), channel_id=1, source_target_pairs={{0,8},{2,10},{4,12},{6,14},{8,0},{10,2},{12,4},{14,6},{16,24},{18,... | collective-permute-start | bytes 393224 | tf_op jit(solution)/shard_map/ppermute | solution.py:191
  57.9 33.5 %collective-permute-start.15 = (bf16[1,1024,128]{2,1,0:T(8,128)(2,1)S(1)}, bf16[1,1024,128]{2,1,0:T(8,128)(2,1)S(1)}, u32[]{:S(2)}, u32[]{:S(2)}) collective-permute-start(bf16[1,1024,128]{2,1,0:T(8,128)(2,1)S(1)} %maximum_select_fusion.11), channel_id=1, source_target_pairs={{0,16},{2,18},{4,20},{6,22},{8,24},{10,26},{12,28},{14,30},{16,0},... | collective-permute-start | bytes 786440 | tf_op jit(solution)/shard_map/ppermute | solution.py:191
  67.0 23.5 %collective-permute-start.7 = (bf16[1,1024,128]{2,1,0:T(8,128)(2,1)S(1)}, bf16[1,1024,128]{2,1,0:T(8,128)(2,1)S(1)}, u32[]{:S(2)}, u32[]{:S(2)}) collective-permute-start(bf16[1,1024,128]{2,1,0:T(8,128)(2,1)S(1)} %maximum_select_fusion.7), channel_id=1, source_target_pairs={{0,16},{2,18},{4,20},{6,22},{8,24},{10,26},{12,28},{14,30},{16,0},... | collective-permute-start | bytes 786440 | tf_op jit(solution)/shard_map/ppermute | solution.py:191
  68.4 25.2 %collective-permute-start.11 = (bf16[1,1024,128]{2,1,0:T(8,128)(2,1)S(1)}, bf16[1,1024,128]{2,1,0:T(8,128)(2,1)S(1)}, u32[]{:S(2)}, u32[]{:S(2)}) collective-permute-start(bf16[1,1024,128]{2,1,0:T(8,128)(2,1)S(1)} %maximum_select_fusion.9), channel_id=1, source_target_pairs={{0,16},{2,18},{4,20},{6,22},{8,24},{10,26},{12,28},{14,30},{16,0},... | collective-permute-start | bytes 786440 | tf_op jit(solution)/shard_map/ppermute | solution.py:191
  102.2 9.2 %copy-start.6 = (f32[128,2,2048]{2,0,1:T(8,128)S(1)}, f32[128,2,2048]{2,0,1:T(8,128)}, u32[]{:S(2)}) copy-start(f32[128,2,2048]{2,0,1:T(8,128)} %copy-done.5) | copy-start | bytes 6291460
  118.5 11.9 %copy-start.22 = (f32[1,128,512]{2,1,0:T(8,128)}, f32[1,128,512]{2,1,0:T(8,128)S(1)}, u32[]{:S(2)}) copy-start(f32[1,128,512]{2,1,0:T(8,128)S(1)} %get-tuple-element.408) | copy-start | bytes 786436
  118.5 11.9 %copy-start.140 = (f32[128]{0:T(128)}, f32[128]{0:T(128)S(1)}, u32[]{:S(2)}) copy-start(f32[128]{0:T(128)S(1)} %broadcast_multiply_fusion.7) | copy-start | bytes 1540
  120.2 10.2 %copy-start.150 = (f32[128]{0:T(128)}, f32[128]{0:T(128)S(1)}, u32[]{:S(2)}) copy-start(f32[128]{0:T(128)S(1)} %fusion.256) | copy-start | bytes 1540
  180.7 154.2 %reduce-scatter.15.cloned.1.call-start = ((), (), s32[]{:S(2)}) async-start(), calls=%async_computation.14 | async-start | bytes 1114112 | tf_op jit(solution)/shard_map/reduce_scatter | solution.py:254
  196.4 9.5 %copy-start.51 = (bf16[128,2,2048]{2,0,1:T(8,128)(2,1)S(1)}, bf16[128,2,2048]{2,0,1:T(8,128)(2,1)}, u32[]{:S(2)}) copy-start(bf16[128,2,2048]{2,0,1:T(8,128)(2,1)} %copy-done.50) | copy-start | bytes 3145732
  196.4 9.5 %copy-start.91 = (f32[128,2,64]{0,2,1:T(8,128)S(1)}, f32[128,2,64]{0,2,1:T(8,128)}, u32[]{:S(2)}) copy-start(f32[128,2,64]{0,2,1:T(8,128)} %copy.278) | copy-start | bytes 196612
  208.0 203.7 %reduce-scatter.13.cloned.1.call-start = ((), (), s32[]{:S(2)}) async-start(), calls=%async_computation.13 | async-start | bytes 1114112 | tf_op jit(solution)/shard_map/reduce_scatter | solution.py:254
  225.9 332.9 %reduce-scatter.11.cloned.1.call-start = ((), (), s32[]{:S(2)}) async-start(), calls=%async_computation.12 | async-start | bytes 1114112 | tf_op jit(solution)/shard_map/reduce_scatter | solution.py:254
  420.7 5.0 collective-permute-start
  426.6 4.3 collective-permute-start.1
  431.7 5.3 collective-permute-start.2
  434.6 13.7 %copy-start.93 = (f32[128,2,64]{0,2,1:T(8,128)S(1)}, f32[128,2,64]{0,2,1:T(8,128)}, u32[]{:S(2)}) copy-start(f32[128,2,64]{0,2,1:T(8,128)} %copy.264) | copy-start | bytes 196612
  438.0 10.1 %collective-permute-start.3 = (bf16[1,1024,128]{2,1,0:T(8,128)(2,1)S(1)}, bf16[1,1024,128]{2,1,0:T(8,128)(2,1)S(1)}, u32[]{:S(2)}, u32[]{:S(2)}) collective-permute-start(bf16[1,1024,128]{2,1,0:T(8,128)(2,1)S(1)} %maximum_select_fusion.5), channel_id=1, source_target_pairs={{0,16},{2,18},{4,20},{6,22},{8,24},{10,26},{12,28},{14,30},{16,0},... | collective-permute-start | bytes 786440 | tf_op jit(solution)/shard_map/ppermute | solution.py:191
  482.9 105.7 %reduce-scatter.19.cloned.1.call-start = ((), (), s32[]{:S(2)}) async-start(), calls=%async_computation.16 | async-start | bytes 12288 | tf_op jit(solution)/shard_map/reduce_scatter | solution.py:297
  493.3 95.4 %reduce-scatter.25.cloned.1.call-start = ((), (), s32[]{:S(2)}) async-start(), calls=%async_computation.19 | async-start | bytes 786432 | tf_op jit(solution)/shard_map/reduce_scatter | solution.py:306
  496.7 91.9 %reduce-scatter.21.cloned.1.call-start = ((), (), s32[]{:S(2)}) async-start(), calls=%async_computation.17 | async-start | bytes 786432 | tf_op jit(solution)/shard_map/reduce_scatter | solution.py:300
  500.1 98.9 %reduce-scatter.23.cloned.1.call-start = ((), (), s32[]{:S(2)}) async-start(), calls=%async_computation.18 | async-start | bytes 196608 | tf_op jit(solution)/shard_map/reduce_scatter | solution.py:303
  504.0 59.8 %copy-start.17 = (f32[1,128,512]{2,1,0:T(8,128)S(1)}, f32[1,128,512]{2,1,0:T(8,128)}, u32[]{:S(2)}) copy-start(f32[1,128,512]{2,1,0:T(8,128)} %copy-done.15) | copy-start | bytes 786436
  563.8 48.8 %reduce-scatter.27.cloned.1.call-start = ((), (), s32[]{:S(2)}) async-start(), calls=%async_computation.20 | async-start | bytes 3145728 | tf_op jit(solution)/shard_map/reduce_scatter | solution.py:312
  570.9 55.2 %reduce-scatter.29.cloned.1.call-start = ((), (), s32[]{:S(2)}) async-start(), calls=%async_computation.21 | async-start | bytes 3145728 | tf_op jit(solution)/shard_map/reduce_scatter | solution.py:315
  586.7 9.8 %copy-start.39 = (bf16[4,128,512]{2,1,0:T(8,128)(2,1)S(1)}, bf16[4,128,512]{2,1,0:T(8,128)(2,1)}, u32[]{:S(2)}) copy-start(bf16[4,128,512]{2,1,0:T(8,128)(2,1)} %param.23) | copy-start | bytes 1572868
  586.7 9.8 %copy-start.58 = (f32[1,128,512]{2,1,0:T(8,128)S(1)}, f32[1,128,512]{2,1,0:T(8,128)}, u32[]{:S(2)}) copy-start(f32[1,128,512]{2,1,0:T(8,128)} %copy-done.57) | copy-start | bytes 786436
  586.7 9.8 %copy-start.60 = (f32[1,128,512]{2,1,0:T(8,128)S(1)}, f32[1,128,512]{2,1,0:T(8,128)}, u32[]{:S(2)}) copy-start(f32[1,128,512]{2,1,0:T(8,128)} %copy-done.59) | copy-start | bytes 786436
  588.7 8.9 %copy-start.54 = (f32[1,128,512]{2,1,0:T(8,128)S(1)}, f32[1,128,512]{2,1,0:T(8,128)}, u32[]{:S(2)}) copy-start(f32[1,128,512]{2,1,0:T(8,128)} %copy-done.52) | copy-start | bytes 786436
  588.7 8.9 %copy-start.56 = (f32[1,128,512]{2,1,0:T(8,128)S(1)}, f32[1,128,512]{2,1,0:T(8,128)}, u32[]{:S(2)}) copy-start(f32[1,128,512]{2,1,0:T(8,128)} %copy-done.55) | copy-start | bytes 786436
  588.7 8.9 %copy-start.131 = (f32[128]{0:T(128)S(1)}, f32[128]{0:T(128)}, u32[]{:S(2)}) copy-start(f32[128]{0:T(128)} %copy-done.130) | copy-start | bytes 1540
  588.7 8.9 %copy-start.132 = (f32[128]{0:T(128)S(1)}, f32[128]{0:T(128)}, u32[]{:S(2)}) copy-start(f32[128]{0:T(128)} %broadcast_multiply_fusion.12) | copy-start | bytes 1540
  588.7 8.9 %copy-start.137 = (f32[128]{0:T(128)S(1)}, f32[128]{0:T(128)}, u32[]{:S(2)}) copy-start(f32[128]{0:T(128)} %copy-done.136) | copy-start | bytes 1540
  597.7 28.5 %copy-start.99 = (bf16[256,512]{1,0:T(8,128)(2,1)S(1)}, bf16[256,512]{1,0:T(8,128)(2,1)}, u32[]{:S(2)}) copy-start(bf16[256,512]{1,0:T(8,128)(2,1)} %reduce-scatter.25.cloned.1.call-done) | copy-start | bytes 786436
  597.7 28.5 %copy-start.100 = (bf16[256,512]{1,0:T(8,128)(2,1)S(1)}, bf16[256,512]{1,0:T(8,128)(2,1)}, u32[]{:S(2)}) copy-start(bf16[256,512]{1,0:T(8,128)(2,1)} %reduce-scatter.21.cloned.1.call-done) | copy-start | bytes 786436
  597.7 28.5 %copy-start.161 = (bf16[256,8]{0,1:T(8,128)(2,1)S(1)}, bf16[256,8]{0,1:T(8,128)(2,1)}, u32[]{:S(2)}) copy-start(bf16[256,8]{0,1:T(8,128)(2,1)} %reduce-scatter.19.cloned.1.call-done) | copy-start | bytes 12292
  (157 other events, 520.9 us)
Sparse Core Ops, SparseCore 0:
  9.6 13.2 all-gather.4
  24.4 11.7 all-gather.6
  180.8 77.0 reduce-scatter.16
  260.7 74.1 reduce-scatter.14
  337.6 74.1 reduce-scatter.12
  483.0 75.6 reduce-scatter.10
  561.5 3.7 reduce-scatter.18
  567.6 9.1 reduce-scatter.24
  579.1 9.0 reduce-scatter.20
  590.3 8.6 reduce-scatter.22
  601.8 10.7 reduce-scatter.26
  615.4 10.7 reduce-scatter.28
